TPU v7x, 128 devices: a whole 4x4x4 slice. The times are simulated.
128 devices in a mesh: rep: 16 (over y, z), grp: 8 (over x, core).
Axes of the slice: x: 4, y: 4, z: 4, core: 2. Of those that a mesh axis runs over, the one named last changes fastest.
Arguments:
- grad_query: float32 [16, 2048, 2048], P('rep', 'grp'), may hold values from -100 to 100, as said below
- error_query: float32 [16, 2048, 2048], P('rep', 'grp'), may hold values from -3 to 3
- basis_query: float32 [2048, 32], replicated, may hold values from -0.125 to 0.125
- momentum_query: float32 [2048, 2048], P('grp'), may hold values from -0.6 to 0.6
- master_query: float32 [2048, 2048], P('grp'), may hold values from -6 to 6
- grad_gate: float32 [16, 2048, 256], P('rep', 'grp'), may hold values from -100 to 100, as said below
- error_gate: float32 [16, 2048, 256], P('rep', 'grp'), may hold values from -3 to 3
- basis_gate: float32 [256, 32], replicated, may hold values from -0.375 to 0.375
- momentum_gate: float32 [2048, 256], P('grp'), may hold values from -0.6 to 0.6
- master_gate: float32 [2048, 256], P('grp'), may hold values from -6 to 6
- vector_grad: float32 [16, 12800], P('rep', 'grp'), may hold values from -6 to 6
- vector_momentum: float32 [12800], P('grp'), may hold values from -0.6 to 0.6
- vector_master: float32 [12800], P('grp'), may hold values from 0.5 to 1.5
Outputs:
- new_error_query: float32 [16, 2048, 2048], P('rep', 'grp')
- new_momentum_query: float32 [2048, 2048], P('grp')
- new_master_query: float32 [2048, 2048], P('grp')
- weight_query: bfloat16 [2048, 2048], replicated
- new_basis_query: float32 [2048, 32], replicated
- new_error_gate: float32 [16, 2048, 256], P('rep', 'grp')
- new_momentum_gate: float32 [2048, 256], P('grp')
- new_master_gate: float32 [2048, 256], P('grp')
- weight_gate: bfloat16 [2048, 256], replicated
- new_basis_gate: float32 [256, 32], replicated
- new_vector_momentum: float32 [12800], P('grp')
- new_vector_master: float32 [12800], P('grp')
- weight_vector: bfloat16 [12800], replicated
Inputs may be any that keep to these rules, and one draw needn't show every extreme that they name: `grad_query`: each replica's gradient is a common part plus a replica's own part. `grad_gate`: each replica's gradient is a common part plus a replica's own part.
All inputs are finite; a program needn't handle non-finite values.
Results may differ from a plain program's by a relative error of at most 0.0006.
Values may be sent and summed in bfloat16 or wider, within the bound.
A program may use at most 128 MiB of HBM per device.

v0:
```python
import jax
import jax.numpy as jnp
from jax import lax
from jax.sharding import PartitionSpec as P

NS_STEPS = 4
highest = lax.Precision.HIGHEST


def inverse_root(gram_matrix):
    trace_value = jnp.trace(gram_matrix)
    identity = jnp.eye(gram_matrix.shape[0], dtype=jnp.float32)
    root_part = gram_matrix / trace_value
    inverse_part = identity
    for iteration in range(NS_STEPS):
        middle = 0.5 * (3.0 * identity - jnp.dot(inverse_part, root_part, precision=highest))
        root_part = jnp.dot(root_part, middle, precision=highest)
        inverse_part = jnp.dot(middle, inverse_part, precision=highest)
    return inverse_part / jnp.sqrt(trace_value)


def right_terms(merged, ortho):
    return jnp.einsum("dn,dr->nr", merged, ortho, precision=highest)


def finish(merged, ortho, new_basis, momentum, master, replicas):
    approx = jnp.dot(ortho, new_basis.T, precision=highest) / replicas
    new_error = (merged - approx)[None]
    new_momentum = 0.9 * momentum + approx
    new_master = master - 0.5 * new_momentum
    return (new_error, new_momentum, new_master)


def per_device(
    grad_query,
    error_query,
    basis_query,
    momentum_query,
    master_query,
    grad_gate,
    error_gate,
    basis_gate,
    momentum_gate,
    master_gate,
    vector_grad,
    vector_momentum,
    vector_master,
):
    replicas = lax.axis_size("rep")
    merged_query = (grad_query + error_query)[0]
    merged_gate = (grad_gate + error_gate)[0]
    local_query = jnp.dot(merged_query, basis_query, precision=highest)
    local_gate = jnp.dot(merged_gate, basis_gate, precision=highest)
    vector_local = vector_grad[0]
    vector_total = lax.psum(vector_local, "rep")
    left_query, left_gate = lax.psum((local_query, local_gate), "rep")
    gram_query, gram_gate = lax.psum(
        (
            jnp.dot(left_query.T, left_query, precision=highest),
            jnp.dot(left_gate.T, left_gate, precision=highest),
        ),
        "grp",
    )
    ortho_query = jnp.dot(left_query, inverse_root(gram_query), precision=highest)
    ortho_gate = jnp.dot(left_gate, inverse_root(gram_gate), precision=highest)
    terms_query = right_terms(merged_query, ortho_query)
    terms_gate = right_terms(merged_gate, ortho_gate)
    basis_new_query, basis_new_gate = lax.psum((terms_query, terms_gate), ("rep", "grp"))
    error_out_query, momentum_out_query, master_out_query = finish(
        merged_query, ortho_query, basis_new_query, momentum_query, master_query, replicas
    )
    error_out_gate, momentum_out_gate, master_out_gate = finish(
        merged_gate, ortho_gate, basis_new_gate, momentum_gate, master_gate, replicas
    )
    vector_mean = vector_total / replicas
    momentum_out_vector = 0.9 * vector_momentum + vector_mean
    master_out_vector = vector_master - 0.5 * momentum_out_vector
    whole_query, whole_gate, whole_vector = (
        lax.all_gather(master_out_query.astype(jnp.bfloat16), "grp", axis=0, tiled=True),
        lax.all_gather(master_out_gate.astype(jnp.bfloat16), "grp", axis=0, tiled=True),
        lax.all_gather(master_out_vector.astype(jnp.bfloat16), "grp", axis=0, tiled=True),
    )
    return (
        error_out_query,
        momentum_out_query,
        master_out_query,
        whole_query,
        basis_new_query,
        error_out_gate,
        momentum_out_gate,
        master_out_gate,
        whole_gate,
        basis_new_gate,
        momentum_out_vector,
        master_out_vector,
        whole_vector,
    )


def solution(mesh):
    in_specs = (
        P("rep", "grp", None),
        P("rep", "grp", None),
        P(),
        P("grp", None),
        P("grp", None),
        P("rep", "grp", None),
        P("rep", "grp", None),
        P(),
        P("grp", None),
        P("grp", None),
        P("rep", "grp"),
        P("grp"),
        P("grp"),
    )
    out_specs = (
        P("rep", "grp", None),
        P("grp", None),
        P("grp", None),
        P(),
        P(),
        P("rep", "grp", None),
        P("grp", None),
        P("grp", None),
        P(),
        P(),
        P("grp"),
        P("grp"),
        P(),
    )
    return jax.shard_map(
        per_device, mesh=mesh, in_specs=in_specs, out_specs=out_specs, check_vma=False
    )
```

profile of v0, /device:TPU:1, one launch (start us, length us, event | category | flops | bytes accessed | tf_op | source)
XLA Modules:
  0.0 369.3 jit_solution(9648238144526546208)
XLA Ops:
  7.2 1.3 reduce
  8.6 4.9 %fusion.2 = f32[256,32]{0,1:T(8,128)} fusion(f32[2048,32]{0,1:T(8,128)S(1)} %copy-done, f32[1,256,2048]{2,1,0:T(8,128)} %param.13, f32[1,256,2048]{2,1,0:T(8,128)} %param.14), kind=kOutput, calls=%fused_computation.4 | convolution fusion | flops 201850880 | bytes 4489216 | tf_op jit(solution)/shard_map/dot_general | solution.py:52
  13.5 1.0 fusion.15
  14.5 83.3 %all-reduce.8.cloned.1.call-done = (f32[256,32]{0,1:T(8,128)}, f32[256,32]{0,1:T(8,128)}, f32[1600]{0:T(1024)}) async-done(((f32[256,32]{0,1:T(8,128)}, f32[256,32]{0,1:T(8,128)}, f32[1600]{0:T(1024)}), (f32[256,32]{0,1:T(8,128)}, f32[256,32]{0,1:T(8,128)}, f32[1600]{0:T(1024)})) %all-reduce.8.cloned.1.call-update) | async-done | bytes 71952 | tf_op jit(solution)/shard_map/psum | solution.py:56
  97.8 1.0 fusion.29
  98.8 1.0 fusion.35
  99.8 22.7 %all-reduce.2 = (f32[32,32]{1,0:T(8,128)S(1)}, f32[32,32]{1,0:T(8,128)S(1)}) all-reduce(f32[32,32]{1,0:T(8,128)S(1)} %fusion.29, f32[32,32]{1,0:T(8,128)S(1)} %fusion.35), channel_id=1, replica_groups=mesh['rep'=16,'grp'=8] {'grp'}, use_global_device_ids=true, to_apply=%region_1.0 | all-reduce | flops 2048 | bytes 16384 | tf_op jit(solution)/shard_map/psum | solution.py:57
  122.5 0.6 select_reduce_fusion
  123.1 0.8 fusion.12
  124.0 0.8 fusion.20
  124.8 0.2 fusion.11
  125.3 0.2 fusion.10
  126.5 0.8 fusion.8
  127.4 0.8 fusion.21
  128.2 0.2 fusion.7
  128.6 0.2 fusion.6
  130.1 1.0 fusion.34
  131.1 3.8 %fusion = f32[2048,32]{0,1:T(8,128)} fusion(f32[256,32]{0,1:T(8,128)S(1)} %fusion.34, f32[1,256,2048]{2,1,0:T(8,128)S(1)} %copy-done.1, f32[1,256,2048]{2,1,0:T(8,128)} %param.14), kind=kOutput, calls=%fused_computation.2 | convolution fusion | flops 201850880 | bytes 4489216 | tf_op jit(solution)/shard_map/dn,dr->nr/dot_general | solution.py:23
  135.3 0.2 fusion.40
  135.5 0.3 fusion.13
  135.8 65.4 %psum.54 = f32[256,32]{0,1:T(8,128)S(1)} all-reduce(f32[256,32]{0,1:T(8,128)S(1)} %fusion.13), channel_id=1, replica_groups=mesh['rep'=16,'grp'=8] {'rep','grp'}, use_global_device_ids=true, to_apply=%region_7.8 | all-reduce | flops 8192 | bytes 65536 | tf_op jit(solution)/shard_map/psum | solution.py:68
  201.2 1.5 fusion.27
  202.8 74.1 %all-reduce.6.cloned.1.call-done = f32[2048,32]{0,1:T(8,128)} async-done(((f32[2048,32]{0,1:T(8,128)}), f32[2048,32]{0,1:T(8,128)}) %all-reduce.6.cloned.1.call-update) | async-done | bytes 262160 | tf_op jit(solution)/shard_map/psum | solution.py:68
  276.8 8.2 %fusion.28 = (bf16[256,2048]{1,0:T(8,128)(2,1)}, f32[256,2048]{1,0:T(8,128)}, f32[256,2048]{1,0:T(8,128)}, f32[1,256,2048]{2,1,0:T(8,128)}) fusion(f32[256,2048]{1,0:T(8,128)} %param.17, f32[256,2048]{1,0:T(8,128)} %param.16, f32[1,256,2048]{2,1,0:T(8,128)S(1)} %copy-done.1, f32[1,256,2048]{2,1,0:T(8,128)} %param.14, f32[256,32]{0,1:T(8,128)S(1)} %fusion.34, ...), kind=kOutput, calls=%fused_computation.53 | convolution fusion | flops 205520896 | bytes 16023552 | tf_op jit(solution)/shard_map/dot_general | solution.py:27
  285.1 0.6 dynamic-slice
  286.4 0.6 fusion.26
  287.0 0.2 dynamic-update-slice
  287.3 22.5 %all-reduce = bf16[12800]{0:T(1024)(128)(2,1)} all-reduce(bf16[12800]{0:T(1024)(128)(2,1)S(1)} %dynamic-update-slice), channel_id=1, replica_groups=mesh['rep'=16,'grp'=8] {'grp'}, use_global_device_ids=true, to_apply=%add | all-reduce | flops 12800 | bytes 51200
  309.7 42.8 %all-gather.3.cloned.1.call-done = bf16[2048,2048]{1,0:T(8,128)(2,1)} async-done(((bf16[256,2048]{1,0:T(8,128)(2,1)}), bf16[2048,2048]{1,0:T(8,128)(2,1)}) %all-gather.3.cloned.1.call-update) | async-done | bytes 8388624 | tf_op jit(solution)/shard_map/all_gather | solution.py:79
  352.5 8.5 %copy.33 = bf16[2048,2048]{1,0:T(8,128)(2,1)} copy(bf16[2048,2048]{1,0:T(8,128)(2,1)} %all-gather.3.cloned.1.call-done) | data formatting | bytes 16777216
  361.1 0.7 copy.34
  361.8 1.0 copy.35
  (54 shorter events, 2.3 us)
Async XLA Ops:
  7.2 1.4 copy-start
  7.2 90.6 %all-reduce.8.cloned.1.call-start = ((), (), s32[]{:S(2)}) async-start(), calls=%async_computation.3 | async-start | bytes 147456 | tf_op jit(solution)/shard_map/psum | solution.py:56
  8.6 4.9 %copy-start.2 = (f32[1,256,256]{2,1,0:T(8,128)S(1)}, f32[1,256,256]{2,1,0:T(8,128)}, u32[]{:S(2)}) copy-start(f32[1,256,256]{2,1,0:T(8,128)} %param.18) | copy-start | bytes 786436
  8.6 4.9 %copy-start.3 = (f32[1,256,256]{2,1,0:T(8,128)S(1)}, f32[1,256,256]{2,1,0:T(8,128)}, u32[]{:S(2)}) copy-start(f32[1,256,256]{2,1,0:T(8,128)} %param.19) | copy-start | bytes 786436
  8.6 4.9 %copy-start.10 = (f32[256,32]{0,1:T(8,128)S(1)}, f32[256,32]{0,1:T(8,128)}, u32[]{:S(2)}) copy-start(f32[256,32]{0,1:T(8,128)} %param.20) | copy-start | bytes 98308
  8.6 122.5 %copy-start.1 = (f32[1,256,2048]{2,1,0:T(8,128)S(1)}, f32[1,256,2048]{2,1,0:T(8,128)}, u32[]{:S(2)}) copy-start(f32[1,256,2048]{2,1,0:T(8,128)} %param.13) | copy-start | bytes 6291460
  14.5 262.4 %all-reduce.6.cloned.1.call-start = ((), (), s32[]{:S(2)}) async-start(), calls=%async_computation | async-start | bytes 524288 | tf_op jit(solution)/shard_map/psum | solution.py:68
  131.1 4.2 %copy-start.6 = (f32[256,32]{0,1:T(8,128)S(1)}, f32[256,32]{0,1:T(8,128)}, u32[]{:S(2)}) copy-start(f32[256,32]{0,1:T(8,128)} %get-tuple-element.14) | copy-start | bytes 98308
  131.1 70.1 %copy-start.7 = (f32[256,256]{1,0:T(8,128)S(1)}, f32[256,256]{1,0:T(8,128)}, u32[]{:S(2)}) copy-start(f32[256,256]{1,0:T(8,128)} %param.22) | copy-start | bytes 786436
  131.1 70.1 %copy-start.8 = (f32[256,256]{1,0:T(8,128)S(1)}, f32[256,256]{1,0:T(8,128)}, u32[]{:S(2)}) copy-start(f32[256,256]{1,0:T(8,128)} %param.21) | copy-start | bytes 786436
  134.9 174.8 %all-gather.5.cloned.1.call-start = ((), (), s32[]{:S(2)}) async-start(), calls=%async_computation.2 | async-start | bytes 1179648 | tf_op jit(solution)/shard_map/all_gather | solution.py:80
  201.2 83.9 %copy-start.9 = (f32[256,32]{0,1:T(8,128)}, f32[256,32]{0,1:T(8,128)S(1)}, u32[]{:S(2)}) copy-start(f32[256,32]{0,1:T(8,128)S(1)} %psum.54) | copy-start | bytes 98308
  202.7 82.5 %copy-start.14 = (u32[128]{0:T(128)S(1)}, u32[128]{0:T(128)}, u32[]{:S(2)}) copy-start(u32[128]{0:T(128)} %constant.33) | copy-start | bytes 1540
  202.7 83.7 %copy-start.11 = (f32[1600]{0:T(1024)S(1)}, f32[1600]{0:T(1024)}, u32[]{:S(2)}) copy-start(f32[1600]{0:T(1024)} %param.25) | copy-start | bytes 19204
  202.7 83.7 %copy-start.12 = (f32[1600]{0:T(1024)S(1)}, f32[1600]{0:T(1024)}, u32[]{:S(2)}) copy-start(f32[1600]{0:T(1024)} %param.24) | copy-start | bytes 19204
  202.7 83.7 %copy-start.13 = (f32[1600]{0:T(1024)S(1)}, f32[1600]{0:T(1024)}, u32[]{:S(2)}) copy-start(f32[1600]{0:T(1024)} %get-tuple-element.15) | copy-start | bytes 19204
  202.7 149.8 %all-gather.3.cloned.1.call-start = ((), (), s32[]{:S(2)}) async-start(), calls=%async_computation.1 | async-start | bytes 9437184 | tf_op jit(solution)/shard_map/all_gather | solution.py:79
  352.5 8.6 %copy-start.4 = (f32[2048,32]{0,1:T(8,128)S(1)}, f32[2048,32]{0,1:T(8,128)}, u32[]{:S(2)}) copy-start(f32[2048,32]{0,1:T(8,128)} %all-reduce.6.cloned.1.call-done) | copy-start | bytes 786436
  352.5 9.3 %copy-start.5 = (bf16[2048,256]{1,0:T(8,128)(2,1)S(1)}, bf16[2048,256]{1,0:T(8,128)(2,1)}, u32[]{:S(2)}) copy-start(bf16[2048,256]{1,0:T(8,128)(2,1)} %all-gather.5.cloned.1.call-done) | copy-start | bytes 3145732
Sparse Core Ops, SparseCore 0:
  14.6 83.1 all-reduce.7
  135.0 141.7 all-reduce.5
  279.3 21.1 all-gather.4
  302.7 49.7 all-gather.2
where the time goes:
time: 370 us; the launch traced here: 369 us
  waiting for transfers between devices  200 us (54%)
  blocking collectives  111 us (30%)
  matrix products  28.5 us (8%)
  between operations  16.1 us (4%)
  local copies, waits for them, and re-layouts  11.1 us (3%)
    psum x1, waiting for transfers between devices, per_device(): left_query, left_gate = lax.psum((local_query, local_gate), 'rep')  83.3 us
    psum x1, waiting for transfers between devices, per_device(): lax.psum((terms_query, terms_gate), ('rep', 'grp'))  74.1 us
    psum x1, blocking collectives, per_device(): lax.psum((terms_query, terms_gate), ('rep', 'grp'))  65.4 us
    all_gather x1, waiting for transfers between devices, per_device(): lax.all_gather(master_out_query.astype(jnp.bfloat16), 'grp', axis=0, tile...  42.8 us
    psum x1, blocking collectives, per_device(): lax.psum((jnp.dot(left_query.T, left_query, precision=highest), jnp.dot(l...  22.7 us
    unnamed x1, blocking collectives  22.5 us
    unnamed x36, local copies, waits for them, and re-layouts  11.1 us
    dot_general x2, matrix products, finish(): approx = jnp.dot(ortho, new_basis.T, precision=highest) / replicas  9.7 us
  transfers between devices with their start and end apart: 4, of which 3 were waited for; matrix products, arithmetic and copies ran while one was open for 3% of the time, Pallas kernels for 0%

commit v1 on v0

--- a/solution.py
+++ b/solution.py
@@ -75,8 +75,17 @@
     vector_mean = vector_total / replicas
     momentum_out_vector = 0.9 * vector_momentum + vector_mean
     master_out_vector = vector_master - 0.5 * momentum_out_vector
+    cut_node = lambda z_in: jnp.concatenate(
+        lax.all_to_all(
+            jnp.stack([z_in for _ in range(lax.psum(1, axis_name="grp"))]),
+            "grp",
+            split_axis=0,
+            concat_axis=0,
+        ),
+        axis=0,
+    )
     whole_query, whole_gate, whole_vector = (
-        lax.all_gather(master_out_query.astype(jnp.bfloat16), "grp", axis=0, tiled=True),
+        cut_node(master_out_query.astype(jnp.bfloat16)),
         lax.all_gather(master_out_gate.astype(jnp.bfloat16), "grp", axis=0, tiled=True),
         lax.all_gather(master_out_vector.astype(jnp.bfloat16), "grp", axis=0, tiled=True),
     )

time: 370 us -> 485 us (1.31)
  blocking collectives: 111 us -> 188 us
  waiting for transfers between devices: 200 us -> 225 us
  starting transfers between devices: 0.16 us -> 6.1 us
    psum x1, blocking collectives: 65.4 us -> 144 us  [per_device(): lax.psum((terms_query, terms_gate), ('rep', 'grp'))]
    psum x1, waiting for transfers between devices: 74.1 us -> 142 us  [per_device(): lax.psum((terms_query, terms_gate), ('rep', 'grp'))]
    all_gather x1 -> x0, waiting for transfers between devices: 42.8 us -> none  [per_device(): lax.all_gather(master_out_query.astype(jnp.bfloat16), 'grp', axis=0, tile...]
    all_to_all x0 -> x1, starting transfers between devices: none -> 5.98 us  [per_device(): lax.all_to_all(jnp.stack([z_in for _ in range(lax.psum(1, axis_name='grp'...]
  transfers between devices with their start and end apart: 4 -> 4, of which waited for: 3 -> 2; matrix products, arithmetic and copies ran while one was open for 3% -> 1% of each run, Pallas kernels for 0% -> 0%
where the time goes in v1:
time: 485 us; the launch traced here: 482 us
  waiting for transfers between devices  225 us (46%)
  blocking collectives  188 us (39%)
  matrix products  28.1 us (6%)
  between operations  16 us (3%)
  local copies, waits for them, and re-layouts  15.6 us (3%)
  starting transfers between devices  6.1 us (1%)
    psum x1, blocking collectives, per_device(): lax.psum((terms_query, terms_gate), ('rep', 'grp'))  144 us
    psum x1, waiting for transfers between devices, per_device(): lax.psum((terms_query, terms_gate), ('rep', 'grp'))  142 us
    psum x1, waiting for transfers between devices, per_device(): left_query, left_gate = lax.psum((local_query, local_gate), 'rep')  83.3 us
    psum x1, blocking collectives, per_device(): lax.psum((jnp.dot(left_query.T, left_query, precision=highest), jnp.dot(l...  22.7 us
    unnamed x1, blocking collectives  22.1 us
    unnamed x36, local copies, waits for them, and re-layouts  11.1 us
  transfers between devices with their start and end apart: 4, of which 2 were waited for; matrix products, arithmetic and copies ran while one was open for 1% of the time, Pallas kernels for 0%

profile of v1, /device:TPU:1, one launch (start us, length us, event | category | flops | bytes accessed | tf_op | source)
XLA Modules:
  0.0 482.1 jit_solution(211546581112215759)
XLA Ops:
  7.2 1.3 reduce
  8.6 4.9 %fusion.2 = f32[256,32]{0,1:T(8,128)} fusion(f32[2048,32]{0,1:T(8,128)S(1)} %copy-done, f32[1,256,2048]{2,1,0:T(8,128)} %param.13, f32[1,256,2048]{2,1,0:T(8,128)} %param.14), kind=kOutput, calls=%fused_computation.4 | convolution fusion | flops 201850880 | bytes 4489216 | tf_op jit(solution)/shard_map/dot_general | solution.py:52
  13.5 1.0 fusion.15
  14.5 83.3 %all-reduce.8.cloned.1.call-done = (f32[256,32]{0,1:T(8,128)}, f32[256,32]{0,1:T(8,128)}, f32[1600]{0:T(1024)}) async-done(((f32[256,32]{0,1:T(8,128)}, f32[256,32]{0,1:T(8,128)}, f32[1600]{0:T(1024)}), (f32[256,32]{0,1:T(8,128)}, f32[256,32]{0,1:T(8,128)}, f32[1600]{0:T(1024)})) %all-reduce.8.cloned.1.call-update) | async-done | bytes 71952 | tf_op jit(solution)/shard_map/psum | solution.py:56
  97.8 1.0 fusion.29
  98.8 1.0 fusion.35
  99.8 22.7 %all-reduce.2 = (f32[32,32]{1,0:T(8,128)S(1)}, f32[32,32]{1,0:T(8,128)S(1)}) all-reduce(f32[32,32]{1,0:T(8,128)S(1)} %fusion.29, f32[32,32]{1,0:T(8,128)S(1)} %fusion.35), channel_id=1, replica_groups=mesh['rep'=16,'grp'=8] {'grp'}, use_global_device_ids=true, to_apply=%region_1.0 | all-reduce | flops 2048 | bytes 16384 | tf_op jit(solution)/shard_map/psum | solution.py:57
  122.5 0.6 select_reduce_fusion
  123.1 0.8 fusion.12
  124.0 0.8 fusion.20
  125.3 0.2 fusion.10
  126.7 1.0 fusion.34
  127.7 3.7 fusion
  131.4 142.0 %all-reduce.6.cloned.1.call-done = f32[2048,32]{0,1:T(8,128)} async-done(((f32[2048,32]{0,1:T(8,128)}), f32[2048,32]{0,1:T(8,128)}) %all-reduce.6.cloned.1.call-update) | async-done | bytes 262160 | tf_op jit(solution)/shard_map/psum | solution.py:68
  273.4 8.0 %fusion.28 = (bf16[256,2048]{1,0:T(8,128)(2,1)S(1)}, f32[256,2048]{1,0:T(8,128)}, f32[256,2048]{1,0:T(8,128)}, f32[1,256,2048]{2,1,0:T(8,128)}) fusion(f32[256,2048]{1,0:T(8,128)} %param.17, f32[256,2048]{1,0:T(8,128)} %param.16, f32[1,256,2048]{2,1,0:T(8,128)S(1)} %copy-done.1, f32[1,256,2048]{2,1,0:T(8,128)} %param.14, f32[256,32]{0,1:T(8,128)S(1)} %fusion.34, ...), kind=kOutput, calls=%fused_computation.53 | convolution fusion | flops 205520896 | bytes 16023552 | tf_op jit(solution)/shard_map/dot_general | solution.py:27
  281.4 4.5 stack.2
  285.9 6.0 %all-to-all-start = ((bf16[8,256,2048]{2,1,0:T(8,128)(2,1)}), bf16[8,256,2048]{2,1,0:T(8,128)(2,1)}, u32[]{:S(2)}, u32[]{:S(2)}) async-start(bf16[8,256,2048]{2,1,0:T(8,128)(2,1)} %stack.2), calls=%async_computation | async-start | bytes 16777216 | tf_op jit(solution)/shard_map/all_to_all | solution.py:79
  292.6 0.8 fusion.8
  293.5 0.8 fusion.21
  294.8 0.2 fusion.6
  295.2 0.2 fusion.5
  295.6 0.2 fusion.40
  295.8 0.3 fusion.13
  296.1 143.6 %psum.54 = f32[256,32]{0,1:T(8,128)S(1)} all-reduce(f32[256,32]{0,1:T(8,128)S(1)} %fusion.13), channel_id=1, replica_groups=mesh['rep'=16,'grp'=8] {'rep','grp'}, use_global_device_ids=true, to_apply=%region_7.8 | all-reduce | flops 8192 | bytes 65536 | tf_op jit(solution)/shard_map/psum | solution.py:68
  439.7 1.4 fusion.27
  441.1 0.6 dynamic-slice
  442.4 0.6 fusion.26
  443.0 0.2 dynamic-update-slice
  443.3 22.1 %all-reduce = bf16[12800]{0:T(1024)(128)(2,1)} all-reduce(bf16[12800]{0:T(1024)(128)(2,1)S(1)} %dynamic-update-slice), channel_id=1, replica_groups=mesh['rep'=16,'grp'=8] {'grp'}, use_global_device_ids=true, to_apply=%add | all-reduce | flops 12800 | bytes 51200
  465.3 8.5 %copy.33 = bf16[2048,2048]{1,0:T(8,128)(2,1)} copy(bf16[2048,2048]{1,0:T(8,128)(2,1)} %bitcast.2) | data formatting | bytes 16777216
  473.9 0.7 copy.34
  474.6 1.0 copy.35
  (54 shorter events, 2.4 us)
Async XLA Ops:
  7.2 1.4 copy-start
  7.2 90.6 %all-reduce.8.cloned.1.call-start = ((), (), s32[]{:S(2)}) async-start(), calls=%async_computation.3 | async-start | bytes 147456 | tf_op jit(solution)/shard_map/psum | solution.py:56
  8.6 4.9 %copy-start.2 = (f32[1,256,256]{2,1,0:T(8,128)S(1)}, f32[1,256,256]{2,1,0:T(8,128)}, u32[]{:S(2)}) copy-start(f32[1,256,256]{2,1,0:T(8,128)} %param.18) | copy-start | bytes 786436
  8.6 4.9 %copy-start.3 = (f32[1,256,256]{2,1,0:T(8,128)S(1)}, f32[1,256,256]{2,1,0:T(8,128)}, u32[]{:S(2)}) copy-start(f32[1,256,256]{2,1,0:T(8,128)} %param.19) | copy-start | bytes 786436
  8.6 4.9 %copy-start.10 = (f32[256,32]{0,1:T(8,128)S(1)}, f32[256,32]{0,1:T(8,128)}, u32[]{:S(2)}) copy-start(f32[256,32]{0,1:T(8,128)} %param.20) | copy-start | bytes 98308
  8.6 119.1 %copy-start.1 = (f32[1,256,2048]{2,1,0:T(8,128)S(1)}, f32[1,256,2048]{2,1,0:T(8,128)}, u32[]{:S(2)}) copy-start(f32[1,256,2048]{2,1,0:T(8,128)} %param.13) | copy-start | bytes 6291460
  14.5 259.0 %all-reduce.6.cloned.1.call-start = ((), (), s32[]{:S(2)}) async-start(), calls=%async_computation.1 | async-start | bytes 524288 | tf_op jit(solution)/shard_map/psum | solution.py:68
  285.9 9.7 %copy-start.6 = (f32[256,32]{0,1:T(8,128)S(1)}, f32[256,32]{0,1:T(8,128)}, u32[]{:S(2)}) copy-start(f32[256,32]{0,1:T(8,128)} %get-tuple-element.14) | copy-start | bytes 98308
  285.9 153.8 %copy-start.7 = (f32[256,256]{1,0:T(8,128)S(1)}, f32[256,256]{1,0:T(8,128)}, u32[]{:S(2)}) copy-start(f32[256,256]{1,0:T(8,128)} %param.22) | copy-start | bytes 786436
  285.9 153.8 %copy-start.8 = (f32[256,256]{1,0:T(8,128)S(1)}, f32[256,256]{1,0:T(8,128)}, u32[]{:S(2)}) copy-start(f32[256,256]{1,0:T(8,128)} %param.21) | copy-start | bytes 786436
  285.9 179.5 %all-to-all-start = ((bf16[8,256,2048]{2,1,0:T(8,128)(2,1)}), bf16[8,256,2048]{2,1,0:T(8,128)(2,1)}, u32[]{:S(2)}, u32[]{:S(2)}) async-start(bf16[8,256,2048]{2,1,0:T(8,128)(2,1)} %stack.2), calls=%async_computation | async-start | bytes 16777216 | tf_op jit(solution)/shard_map/all_to_all | solution.py:79
  291.8 149.3 %copy-start.14 = (u32[128]{0:T(128)S(1)}, u32[128]{0:T(128)}, u32[]{:S(2)}) copy-start(u32[128]{0:T(128)} %constant.33) | copy-start | bytes 1540
  291.8 150.5 %copy-start.11 = (f32[1600]{0:T(1024)S(1)}, f32[1600]{0:T(1024)}, u32[]{:S(2)}) copy-start(f32[1600]{0:T(1024)} %param.25) | copy-start | bytes 19204
  291.9 150.5 %copy-start.12 = (f32[1600]{0:T(1024)S(1)}, f32[1600]{0:T(1024)}, u32[]{:S(2)}) copy-start(f32[1600]{0:T(1024)} %param.24) | copy-start | bytes 19204
  291.9 150.6 %copy-start.13 = (f32[1600]{0:T(1024)S(1)}, f32[1600]{0:T(1024)}, u32[]{:S(2)}) copy-start(f32[1600]{0:T(1024)} %get-tuple-element.15) | copy-start | bytes 19204
  291.9 173.5 %all-gather.2.cloned.1.call-start = ((), (), s32[]{:S(2)}) async-start(), calls=%async_computation.2 | async-start | bytes 1179648 | tf_op jit(solution)/shard_map/all_gather | solution.py:89
  439.7 34.2 %copy-start.9 = (f32[256,32]{0,1:T(8,128)}, f32[256,32]{0,1:T(8,128)S(1)}, u32[]{:S(2)}) copy-start(f32[256,32]{0,1:T(8,128)S(1)} %psum.54) | copy-start | bytes 98308
  465.3 8.6 %copy-start.4 = (f32[2048,32]{0,1:T(8,128)S(1)}, f32[2048,32]{0,1:T(8,128)}, u32[]{:S(2)}) copy-start(f32[2048,32]{0,1:T(8,128)} %all-reduce.6.cloned.1.call-done) | copy-start | bytes 786436
  465.3 9.3 %copy-start.5 = (bf16[2048,256]{1,0:T(8,128)(2,1)S(1)}, bf16[2048,256]{1,0:T(8,128)(2,1)}, u32[]{:S(2)}) copy-start(bf16[2048,256]{1,0:T(8,128)(2,1)} %all-gather.2.cloned.1.call-done) | copy-start | bytes 3145732
Sparse Core Ops, SparseCore 0:
  14.6 83.1 all-reduce.7
  131.6 141.8 all-reduce.5
  441.3 20.4 all-gather.1
